TPU v7x, 128 devices: a whole 4x4x4 slice. The times are simulated.
128 devices in a mesh: req: 32 (over y, x, core), head: 4 (over z).
Axes of the slice: x: 4, y: 4, z: 4, core: 2. Of those that a mesh axis runs over, the one named last changes fastest.
Arguments:
- hidden_in: bfloat16 [1024, 5120], P('req'), may hold values from -60 to 60
- query: bfloat16 [1024, 4096], P('req', 'head'), may hold values from -12 to 12
- incoming_key: bfloat16 [1024, 1024], P('req', 'head'), may hold values from -6 to 6
- incoming_value: bfloat16 [1024, 1024], P('req', 'head'), may hold values from -6 to 6
- private_tail_keys: bfloat16 [1024, 160, 1024], P('req', None, 'head'), may hold values from -6 to 6
- private_tail_values: bfloat16 [1024, 160, 1024], P('req', None, 'head'), may hold values from -6 to 6
- group_prompt_keys: bfloat16 [96, 512, 1024], P('req', None, 'head'), may hold values from -6 to 6
- group_prompt_values: bfloat16 [96, 512, 1024], P('req', None, 'head'), may hold values from -6 to 6
- group_id: int32 [1024], P('req'), may hold values from 0 to 95, as said below
- prompt_len: int32 [96], P('req'), may hold values from 128 to 512, as said below
- tail_len: int32 [1024], P('req'), may hold values from 0 to 159, as said below
- out_proj: bfloat16 [4096, 5120], P('head'), may hold values from -0.5 to 0.5
- norm_gain: float32 [5120], replicated, may hold values from 0.1 to 1.9
- gate_proj: bfloat16 [5120, 32768], P(None, ('req', 'head')), may hold values from -0.078125 to 0.078125
- up_proj: bfloat16 [5120, 32768], P(None, ('req', 'head')), may hold values from -0.078125 to 0.078125
- down_proj: bfloat16 [32768, 5120], P('req', 'head'), may hold values from -0.03125 to 0.03125
Outputs:
- layer_out: bfloat16 [1024, 5120], P(('req', 'head'))
Inputs may be any that keep to these rules, and one draw needn't show every extreme that they name: `group_id`: the prompt cache of group g is held by index g // 3 of req. Among the 32 requests of one index of req, at most 2 belong to groups held by any one index of req; in every draw one index of req holds the groups of exactly 2 requests of every index of req. `prompt_len`: some group's prompt fills all 512 positions. Request r's earlier private tokens are in slots 0 to tail_len[r] - 1; some request has 159 of them.
All inputs are finite; a program needn't handle non-finite values.
Results may differ from a plain program's by a relative error of at most 0.007.
Values may be sent and summed in bfloat16 or wider, within the bound.
No kernel may reach another device: no remote copies, remote signals or barrier semaphores. Data moves between devices by JAX's collectives and lax.ppermute only.
A program may use at most 128 MiB of HBM per device.

v0:
```python
import jax
import jax.numpy as jnp
from jax import lax
from jax.sharding import PartitionSpec as P

QUERY_HEADS = 32
KEY_VALUE_HEADS = 8
HEAD_WIDTH = 128
MASKED_SCORE = -1e30


def shards(
    hidden_in,
    query,
    incoming_key,
    incoming_value,
    private_tail_keys,
    private_tail_values,
    group_prompt_keys,
    group_prompt_values,
    group_id,
    prompt_len,
    tail_len,
    out_proj,
    norm_gain,
    gate_proj,
    up_proj,
    down_proj,
):
    n_req = lax.axis_size("req")
    n_head = lax.axis_size("head")
    row_count = query.shape[0]
    kv_local = incoming_key.shape[1] // HEAD_WIDTH
    each_key_value = QUERY_HEADS // KEY_VALUE_HEADS
    group_count = prompt_len.shape[0]
    prompt_size = group_prompt_keys.shape[1]
    tail_size = private_tail_keys.shape[1]
    slot_cap = 2 * row_count // n_req
    slot_total = n_req * slot_cap
    scale_of_scores = HEAD_WIDTH ** (-0.5)
    col_width = query.shape[1]
    head_local = kv_local * each_key_value
    holder = group_id // group_count
    local_group = group_id - holder * group_count
    holder_hot = (holder[:, None] == jnp.arange(n_req)[None, :]).astype(jnp.int32)
    before = jnp.cumsum(holder_hot, axis=0) - holder_hot
    order_in = jnp.sum(before * holder_hot, axis=1)
    slot_of = holder * slot_cap + order_in
    placing = slot_of[:, None] == jnp.arange(slot_total)[None, :]
    send_query = (
        jnp.einsum(
            "rs,rc->sc", placing.astype(jnp.bfloat16), query, preferred_element_type=jnp.float32
        )
        .astype(jnp.bfloat16)
        .reshape(n_req, slot_cap, col_width)
    )
    send_group = (
        jnp.sum(placing.astype(jnp.int32) * (local_group[:, None] + 1), axis=0) - 1
    ).reshape(n_req, slot_cap)
    keys_all = group_prompt_keys.reshape(group_count * prompt_size, kv_local, HEAD_WIDTH)
    values_all = group_prompt_values.reshape(group_count * prompt_size, kv_local, HEAD_WIDTH)
    key_group = jnp.arange(group_count * prompt_size) // prompt_size
    key_live = jnp.arange(group_count * prompt_size) % prompt_size < jnp.repeat(
        prompt_len, prompt_size
    )
    recv_query = lax.all_to_all(send_query, "req", split_axis=0, concat_axis=0, tiled=True)
    recv_group = lax.all_to_all(send_group, "req", split_axis=0, concat_axis=0, tiled=True)
    sources, item_count = recv_group.shape
    flat_query = recv_query.reshape(sources * item_count, kv_local, each_key_value, HEAD_WIDTH)
    scores = (
        jnp.einsum("nkrd,pkd->nkrp", flat_query, keys_all, preferred_element_type=jnp.float32)
        * scale_of_scores
    )
    usable = (recv_group.reshape(sources * item_count)[:, None] == key_group[None, :]) & key_live[
        None, :
    ]
    masked = jnp.where(usable[:, None, None, :], scores, MASKED_SCORE)
    largest = jnp.max(masked, axis=-1)
    weights = jnp.exp(masked - largest[..., None])
    totals = jnp.sum(weights, axis=-1)
    mixture = jnp.einsum(
        "nkrp,pkd->nkrd",
        weights.astype(jnp.bfloat16),
        values_all,
        preferred_element_type=jnp.float32,
    )
    back_mix = lax.all_to_all(
        mixture.reshape(sources, item_count, col_width),
        "req",
        split_axis=0,
        concat_axis=0,
        tiled=True,
    )
    back_peak = lax.all_to_all(
        largest.reshape(sources, item_count, head_local),
        "req",
        split_axis=0,
        concat_axis=0,
        tiled=True,
    )
    back_total = lax.all_to_all(
        totals.reshape(sources, item_count, head_local),
        "req",
        split_axis=0,
        concat_axis=0,
        tiled=True,
    )
    shared_mix = jnp.take(back_mix.reshape(slot_total, col_width), slot_of, axis=0).reshape(
        row_count, kv_local, each_key_value, HEAD_WIDTH
    )
    shared_max = jnp.take(back_peak.reshape(slot_total, head_local), slot_of, axis=0).reshape(
        row_count, kv_local, each_key_value
    )
    shared_total = jnp.take(back_total.reshape(slot_total, head_local), slot_of, axis=0).reshape(
        row_count, kv_local, each_key_value
    )
    query_rows = query.reshape(row_count, kv_local, each_key_value, HEAD_WIDTH)
    request_keys = private_tail_keys.reshape(row_count, tail_size, kv_local, HEAD_WIDTH)
    request_values = private_tail_values.reshape(row_count, tail_size, kv_local, HEAD_WIDTH)
    tail_scores = (
        jnp.einsum("bkrd,btkd->bkrt", query_rows, request_keys, preferred_element_type=jnp.float32)
        * scale_of_scores
    )
    current_scores = (
        jnp.einsum(
            "ivxg,ivg->ivx",
            query_rows,
            incoming_key.reshape(row_count, kv_local, HEAD_WIDTH),
            preferred_element_type=jnp.float32,
        )
        * scale_of_scores
    )
    tail_live = (jnp.arange(tail_size)[None, :] < tail_len[:, None])[:, None, None, :]
    tail_masked = jnp.where(tail_live, tail_scores, MASKED_SCORE)
    local_max = jnp.maximum(jnp.max(tail_masked, axis=-1), current_scores)
    tail_exp = jnp.exp(tail_masked - local_max[..., None])
    fresh_exp = jnp.exp(current_scores - local_max)
    local_total = jnp.sum(tail_exp, axis=-1) + fresh_exp
    fresh_weights = lax.optimization_barrier(fresh_exp.astype(jnp.bfloat16)).astype(jnp.float32)
    fresh_vals = incoming_value.reshape(row_count, kv_local, HEAD_WIDTH).astype(jnp.float32)
    local_mix = (
        jnp.einsum(
            "bkrt,btkd->bkrd",
            tail_exp.astype(jnp.bfloat16),
            request_values,
            preferred_element_type=jnp.float32,
        )
        + fresh_weights[..., None] * fresh_vals[:, :, None, :]
    )
    highest = jnp.maximum(shared_max, local_max)
    shared_factor = jnp.exp(shared_max - highest)
    local_factor = jnp.exp(local_max - highest)
    numer = shared_mix * shared_factor[..., None] + local_mix * local_factor[..., None]
    denom = shared_total * shared_factor + local_total * local_factor
    attention = (numer / denom[..., None]).reshape(row_count, col_width).astype(jnp.bfloat16)
    projected = jnp.dot(attention, out_proj, preferred_element_type=jnp.float32)
    sub_rows = row_count // n_head
    head_index = lax.axis_index("head")
    summed = lax.psum(projected, "head")
    residual = (hidden_in.astype(jnp.float32) + summed).astype(jnp.bfloat16)
    resid_f = residual.astype(jnp.float32)
    segment = lax.all_gather(
        (
            resid_f
            * lax.rsqrt(jnp.mean(resid_f * resid_f, axis=-1, keepdims=True) + 1e-05)
            * norm_gain
        ).astype(jnp.bfloat16),
        "req",
        axis=0,
        tiled=True,
    )
    gate_vals = jnp.dot(segment, gate_proj, preferred_element_type=jnp.float32)
    up_vals = jnp.dot(segment, up_proj, preferred_element_type=jnp.float32)
    hidden = (jax.nn.silu(gate_vals) * up_vals).astype(jnp.bfloat16)
    own_rows = lax.dynamic_slice_in_dim(residual, head_index * sub_rows, sub_rows, 0)
    down_rows = lax.all_to_all(down_proj, "head", split_axis=0, concat_axis=1, tiled=True)
    lowered = lax.psum_scatter(
        jnp.dot(hidden, down_rows, preferred_element_type=jnp.float32),
        ("req", "head"),
        scatter_dimension=0,
        tiled=True,
    )
    return (own_rows.astype(jnp.float32) + lowered).astype(jnp.bfloat16)


def solution(mesh):
    return jax.shard_map(
        shards,
        mesh=mesh,
        in_specs=(
            P("req", None),
            P("req", "head"),
            P("req", "head"),
            P("req", "head"),
            P("req", None, "head"),
            P("req", None, "head"),
            P("req", None, "head"),
            P("req", None, "head"),
            P("req"),
            P("req"),
            P("req"),
            P("head", None),
            P(),
            P(None, ("req", "head")),
            P(None, ("req", "head")),
            P("req", "head"),
        ),
        out_specs=P(("req", "head"), None),
        check_vma=False,
    )
```

profile of v0, /device:TPU:0, one launch (start us, length us, event | category | flops | bytes accessed | tf_op | source)
XLA Modules:
  0.0 910.8 jit_solution(5117704881106043649)
XLA Ops:
  9.0 7.4 all-to-all-start
  20.5 3.3 fusion.65
  27.1 2.0 reshape.202
  29.2 7.5 all-to-all-start.1
  38.8 5.7 all-to-all-done.1
  44.5 1.6 reshape.201
  46.1 1.7 fusion.66
  51.0 3.9 all-to-all-start.4
  55.5 2.0 reshape.203
  59.8 2.5 all-to-all-done.4
  62.2 4.9 all-to-all-start.3
  67.2 2.6 fusion.20
  71.5 3.0 all-to-all-done.3
  74.6 4.4 all-to-all-start.2
  82.0 5.8 all-to-all-done.2
  88.9 2.6 fusion.35
  91.6 6.8 fusion.68
  98.6 42.6 %all-reduce.2.cloned.1.call-done = f32[32,5120]{1,0:T(8,128)} async-done(((f32[32,5120]{1,0:T(8,128)}), f32[32,5120]{1,0:T(8,128)}) %all-reduce.2.cloned.1.call-update) | async-done | bytes 655376 | tf_op jit(solution)/shard_map/psum | solution.py:159
  143.4 35.0 %all_to_all.45 = bf16[4,256,1280]{2,1,0:T(8,128)(2,1)} all-to-all(bf16[4,256,1280]{2,1,0:T(8,128)(2,1)} %bitcast.79), channel_id=1, replica_groups=mesh['req'=32,'head'=4] {'head'}, dimensions={0} | all-to-all | bytes 5242880 | tf_op jit(solution)/shard_map/all_to_all | solution.py:176
  178.4 4.4 copy.99
  182.8 19.0 %all-gather.2.cloned.1.call-done = bf16[1024,5120]{1,0:T(8,128)(2,1)} async-done(((bf16[32,5120]{1,0:T(8,128)(2,1)}), bf16[1024,5120]{1,0:T(8,128)(2,1)}) %all-gather.2.cloned.1.call-update) | async-done | bytes 10485776 | tf_op jit(solution)/shard_map/all_gather | solution.py:162
  201.8 8.6 fusion.69
  210.4 18.4 %fusion.70 = f32[1024,5120]{1,0:T(8,128)} fusion(bf16[256,5120]{0,1:T(8,128)(2,1)} %bitcast.75, bf16[1024,5120]{1,0:T(8,128)(2,1)} %all-gather.2.cloned.1.call-done, bf16[5120,256]{1,0:T(8,128)(2,1)S(1)} %copy-done, f32[1024,256]{1,0:T(8,128)} %fusion.69), kind=kOutput, calls=%fused_computation.86 | convolution fusion | flops 5370281984 | bytes 37748736 | tf_op jit(solution)/shard_map/dot_general | solution.py:178
  228.8 673.9 %reduce-scatter.2.cloned.1.call-done = f32[8,5120]{1,0:T(8,128)} async-done(((f32[1024,5120]{1,0:T(8,128)}), f32[8,5120]{1,0:T(8,128)}) %reduce-scatter.2.cloned.1.call-update) | async-done | bytes 163856 | tf_op jit(solution)/shard_map/reduce_scatter | solution.py:177
  (87 shorter events, 27.8 us)
Async XLA Ops:
  6.5 203.8 %copy-start = (bf16[5120,256]{1,0:T(8,128)(2,1)S(1)}, bf16[5120,256]{1,0:T(8,128)(2,1)}, u32[]{:S(2)}) copy-start(bf16[5120,256]{1,0:T(8,128)(2,1)} %param.32) | copy-start | bytes 7864324
  6.5 17.4 %copy-start.8 = (bf16[32,256]{1,0:T(8,128)(2,1)S(1)}, bf16[32,256]{1,0:T(8,128)(2,1)}, u32[]{:S(2)}) copy-start(bf16[32,256]{1,0:T(8,128)(2,1)} %param.20) | copy-start | bytes 49156
  9.0 20.1 %all-to-all-start = ((s32[32,1,2]{2,1,0:T(1,128)}), s32[32,1,2]{2,1,0:T(1,128)S(1)}, u32[]{:S(2)}, u32[]{:S(2)}) async-start(s32[32,1,2]{2,1,0:T(1,128)} %bitcast), calls=%async_computation | async-start | bytes 32768 | tf_op jit(solution)/shard_map/all_to_all | solution.py:67
  23.8 2.6 copy-start.4
  29.2 15.3 %all-to-all-start.1 = ((bf16[32,2,1024]{2,1,0:T(2,128)(2,1)}), bf16[32,2,1024]{2,1,0:T(2,128)(2,1)}, u32[]{:S(2)}, u32[]{:S(2)}) async-start(bf16[32,2,1024]{2,1,0:T(2,128)(2,1)} %reshape.200), calls=%async_computation.1 | async-start | bytes 262144 | tf_op jit(solution)/shard_map/all_to_all | solution.py:66
  47.8 1.7 copy-start.2
  47.8 7.0 copy-start.11
  47.8 7.6 copy-start.6
  47.9 9.7 %copy-start.10 = (bf16[32,2,4]{0,2,1:T(4,128)(2,1)S(1)}, bf16[32,2,4]{0,2,1:T(4,128)(2,1)}, u32[]{:S(2)}) copy-start(bf16[32,2,4]{0,2,1:T(4,128)(2,1)} %get-tuple-element.8) | copy-start | bytes 1540
  47.9 10.4 %copy-start.9 = (bf16[32,256]{1,0:T(8,128)(2,1)S(1)}, bf16[32,256]{1,0:T(8,128)(2,1)}, u32[]{:S(2)}) copy-start(bf16[32,256]{1,0:T(8,128)(2,1)} %param.21) | copy-start | bytes 49156
  51.0 11.3 %all-to-all-start.4 = ((f32[32,2,8]{2,1,0:T(2,128)}), f32[32,2,8]{2,1,0:T(2,128)S(1)}, u32[]{:S(2)}, u32[]{:S(2)}) async-start(f32[32,2,8]{2,1,0:T(2,128)} %reshape.213), calls=%async_computation.4 | async-start | bytes 65536 | tf_op jit(solution)/shard_map/all_to_all | solution.py:101
  62.2 12.3 %all-to-all-start.3 = ((f32[32,2,8]{2,1,0:T(2,128)}), f32[32,2,8]{2,1,0:T(2,128)S(1)}, u32[]{:S(2)}, u32[]{:S(2)}) async-start(f32[32,2,8]{2,1,0:T(2,128)} %reshape.206), calls=%async_computation.3 | async-start | bytes 65536 | tf_op jit(solution)/shard_map/all_to_all | solution.py:94
  69.8 19.1 %copy-start.5 = (f32[32,2,4,160]{3,2,1,0:T(4,128)S(1)}, f32[32,2,4,160]{3,2,1,0:T(4,128)}, u32[]{:S(2)}) copy-start(f32[32,2,4,160]{3,2,1,0:T(4,128)} %copy-done.4) | copy-start | bytes 491524
  74.6 13.3 %all-to-all-start.2 = ((f32[32,2,1024]{2,1,0:T(2,128)}), f32[32,2,1024]{2,1,0:T(2,128)S(1)}, u32[]{:S(2)}, u32[]{:S(2)}) async-start(f32[32,2,1024]{2,1,0:T(2,128)} %reshape.204), calls=%async_computation.2 | async-start | bytes 524288 | tf_op jit(solution)/shard_map/all_to_all | solution.py:87
  78.9 62.2 %all-reduce.2.cloned.1.call-start = ((), (), s32[]{:S(2)}) async-start(), calls=%async_computation.7 | async-start | bytes 1310720 | tf_op jit(solution)/shard_map/psum | solution.py:159
  91.5 49.6 %copy-start.3 = (bf16[32,5120]{1,0:T(8,128)(2,1)S(1)}, bf16[32,5120]{1,0:T(8,128)(2,1)}, u32[]{:S(2)}) copy-start(bf16[32,5120]{1,0:T(8,128)(2,1)} %param.18) | copy-start | bytes 983044
  91.5 50.9 %copy-start.7 = (f32[5120]{0:T(1024)S(1)}, f32[5120]{0:T(1024)}, u32[]{:S(2)}) copy-start(f32[5120]{0:T(1024)} %param.30) | copy-start | bytes 61444
  98.4 103.4 %all-gather.2.cloned.1.call-start = ((), (), s32[]{:S(2)}) async-start(), calls=%async_computation.8 | async-start | bytes 10813440 | tf_op jit(solution)/shard_map/all_gather | solution.py:162
  143.4 759.3 %reduce-scatter.2.cloned.1.call-start = ((), (), s32[]{:S(2)}) async-start(), calls=%async_computation.9 | async-start | bytes 21135360 | tf_op jit(solution)/shard_map/reduce_scatter | solution.py:177
  228.8 675.5 %copy-start.1 = (bf16[5120,256]{1,0:T(8,128)(2,1)S(1)}, bf16[5120,256]{1,0:T(8,128)(2,1)}, u32[]{:S(2)}) copy-start(bf16[5120,256]{1,0:T(8,128)(2,1)} %param.32) | copy-start | bytes 7864324
Sparse Core Ops, SparseCore 0:
  98.5 42.6 all-reduce.1
  143.5 58.2 all-gather.1
  229.0 673.7 reduce-scatter.1
where the time goes:
time: 912 us; the launch traced here: 911 us
  waiting for transfers between devices  753 us (83%)
  matrix products  45.3 us (5%)
  blocking collectives  35 us (4%)
  starting transfers between devices  28.4 us (3%)
  local copies, waits for them, and re-layouts  23.9 us (3%)
  between operations  13.4 us (1%)
  other arithmetic  12.3 us (1%)
    reduce_scatter x1, waiting for transfers between devices, shards(): lax.psum_scatter(jnp.dot(hidden, down_rows, preferred_element_type=jnp.fl...  674 us
    psum x1, waiting for transfers between devices, shards(): summed = lax.psum(projected, 'head')  42.6 us
    all_to_all x1, blocking collectives, shards(): lax.all_to_all(down_proj, 'head', split_axis=0, concat_axis=1, tiled=True)  35 us
    all_gather x1, waiting for transfers between devices, shards(): lax.all_gather((resid_f * lax.rsqrt(jnp.mean(resid_f * resid_f, axis=-1,...  19 us
    dot_general x1, matrix products, shards(): jnp.dot(hidden, down_rows, preferred_element_type=jnp.float32)  18.4 us
  transfers between devices with their start and end apart: 8, of which 7 were waited for; matrix products, arithmetic and copies ran while one was open for 3% of the time, Pallas kernels for 0%

commit v1 on v0

--- a/solution.py
+++ b/solution.py
@@ -7,6 +7,7 @@
 KEY_VALUE_HEADS = 8
 HEAD_WIDTH = 128
 MASKED_SCORE = -1e30
+place_fields_over_axis = lambda work_x, mesh_name: jnp.sum(lax.all_gather(work_x, mesh_name), 0)
 
 
 def shards(
@@ -156,7 +157,7 @@
     projected = jnp.dot(attention, out_proj, preferred_element_type=jnp.float32)
     sub_rows = row_count // n_head
     head_index = lax.axis_index("head")
-    summed = lax.psum(projected, "head")
+    summed = place_fields_over_axis(projected, "head")
     residual = (hidden_in.astype(jnp.float32) + summed).astype(jnp.bfloat16)
     resid_f = residual.astype(jnp.float32)
     segment = lax.all_gather(

time: 912 us -> 906 us (level)
  waiting for transfers between devices: 753 us -> 742 us
    psum x1 -> x0, waiting for transfers between devices: 42.6 us -> none  [shards(): summed = lax.psum(projected, 'head')]
    all_gather x0 -> x1, waiting for transfers between devices: none -> 34.2 us  [lax.all_gather(work_x, mesh_name)]
where the time goes in v1:
time: 906 us; the launch traced here: 905 us
  waiting for transfers between devices  742 us (82%)
  matrix products  45.3 us (5%)
  blocking collectives  36.7 us (4%)
  starting transfers between devices  28.4 us (3%)
  local copies, waits for them, and re-layouts  24.7 us (3%)
  other arithmetic  14.2 us (2%)
  between operations  13.4 us (1%)
    reduce_scatter x1, waiting for transfers between devices, shards(): lax.psum_scatter(jnp.dot(hidden, down_rows, preferred_element_type=jnp.fl...  674 us
    all_to_all x1, blocking collectives, shards(): lax.all_to_all(down_proj, 'head', split_axis=0, concat_axis=1, tiled=True)  36.7 us
    all_gather x1, waiting for transfers between devices, lax.all_gather(work_x, mesh_name)  34.2 us
    dot_general x1, matrix products, shards(): jnp.dot(hidden, down_rows, preferred_element_type=jnp.float32)  18.4 us
  transfers between devices with their start and end apart: 8, of which 7 were waited for; matrix products, arithmetic and copies ran while one was open for 3% of the time, Pallas kernels for 0%

profile of v1, /device:TPU:0, one launch (start us, length us, event | category | flops | bytes accessed | tf_op | source)
XLA Modules:
  0.0 904.8 jit_solution(4670169929956758651)
XLA Ops:
  9.0 7.4 all-to-all-start
  20.5 3.3 fusion.65
  27.1 2.0 reshape.202
  29.2 7.5 all-to-all-start.1
  38.8 5.7 all-to-all-done.1
  46.1 1.7 fusion.66
  51.0 3.9 all-to-all-start.4
  55.5 2.0 reshape.203
  59.8 2.5 all-to-all-done.4
  62.2 4.9 all-to-all-start.3
  67.2 2.6 fusion.20
  71.5 3.0 all-to-all-done.3
  74.6 4.4 all-to-all-start.2
  82.0 5.8 all-to-all-done.2
  88.9 2.6 fusion.35
  91.5 6.7 fusion.68
  98.5 34.2 %all-gather.6.cloned.1.call-done = f32[128,5120]{1,0:T(8,128)} async-done(((f32[32,5120]{1,0:T(8,128)}), f32[128,5120]{1,0:T(8,128)}) %all-gather.6.cloned.1.call-update) | async-done | bytes 2621456 | tf_op jit(solution)/shard_map/all_gather | solution.py:10
  132.7 2.0 reduce_sum.58
  137.5 36.7 %all_to_all.45 = bf16[4,256,1280]{2,1,0:T(8,128)(2,1)} all-to-all(bf16[4,256,1280]{2,1,0:T(8,128)(2,1)} %bitcast.80), channel_id=1, replica_groups=mesh['req'=32,'head'=4] {'head'}, dimensions={0} | all-to-all | bytes 5242880 | tf_op jit(solution)/shard_map/all_to_all | solution.py:177
  174.2 4.5 copy.99
  178.7 16.5 %all-gather.4.cloned.1.call-done = bf16[1024,5120]{1,0:T(8,128)(2,1)} async-done(((bf16[32,5120]{1,0:T(8,128)(2,1)}), bf16[1024,5120]{1,0:T(8,128)(2,1)}) %all-gather.4.cloned.1.call-update) | async-done | bytes 10485776 | tf_op jit(solution)/shard_map/all_gather | solution.py:163
  195.2 8.6 fusion.69
  203.8 18.4 %fusion.70 = f32[1024,5120]{1,0:T(8,128)} fusion(bf16[256,5120]{0,1:T(8,128)(2,1)} %bitcast.76, bf16[1024,5120]{1,0:T(8,128)(2,1)} %all-gather.4.cloned.1.call-done, bf16[5120,256]{1,0:T(8,128)(2,1)S(1)} %copy-done, f32[1024,256]{1,0:T(8,128)} %fusion.69), kind=kOutput, calls=%fused_computation.86 | convolution fusion | flops 5370281984 | bytes 37748736 | tf_op jit(solution)/shard_map/dot_general | solution.py:179
  222.3 674.4 %reduce-scatter.2.cloned.1.call-done = f32[8,5120]{1,0:T(8,128)} async-done(((f32[1024,5120]{1,0:T(8,128)}), f32[8,5120]{1,0:T(8,128)}) %reduce-scatter.2.cloned.1.call-update) | async-done | bytes 163856 | tf_op jit(solution)/shard_map/reduce_scatter | solution.py:178
  (88 shorter events, 30.1 us)
Async XLA Ops:
  6.5 197.3 %copy-start = (bf16[5120,256]{1,0:T(8,128)(2,1)S(1)}, bf16[5120,256]{1,0:T(8,128)(2,1)}, u32[]{:S(2)}) copy-start(bf16[5120,256]{1,0:T(8,128)(2,1)} %param.32) | copy-start | bytes 7864324
  6.5 17.4 %copy-start.8 = (bf16[32,256]{1,0:T(8,128)(2,1)S(1)}, bf16[32,256]{1,0:T(8,128)(2,1)}, u32[]{:S(2)}) copy-start(bf16[32,256]{1,0:T(8,128)(2,1)} %param.20) | copy-start | bytes 49156
  9.0 20.1 %all-to-all-start = ((s32[32,1,2]{2,1,0:T(1,128)}), s32[32,1,2]{2,1,0:T(1,128)S(1)}, u32[]{:S(2)}, u32[]{:S(2)}) async-start(s32[32,1,2]{2,1,0:T(1,128)} %bitcast), calls=%async_computation | async-start | bytes 32768 | tf_op jit(solution)/shard_map/all_to_all | solution.py:68
  23.8 2.6 copy-start.4
  29.2 15.3 %all-to-all-start.1 = ((bf16[32,2,1024]{2,1,0:T(2,128)(2,1)}), bf16[32,2,1024]{2,1,0:T(2,128)(2,1)}, u32[]{:S(2)}, u32[]{:S(2)}) async-start(bf16[32,2,1024]{2,1,0:T(2,128)(2,1)} %reshape.200), calls=%async_computation.1 | async-start | bytes 262144 | tf_op jit(solution)/shard_map/all_to_all | solution.py:67
  47.8 1.7 copy-start.2
  47.8 7.0 copy-start.11
  47.8 7.6 copy-start.6
  47.9 9.7 %copy-start.10 = (bf16[32,2,4]{0,2,1:T(4,128)(2,1)S(1)}, bf16[32,2,4]{0,2,1:T(4,128)(2,1)}, u32[]{:S(2)}) copy-start(bf16[32,2,4]{0,2,1:T(4,128)(2,1)} %get-tuple-element.8) | copy-start | bytes 1540
  47.9 10.4 %copy-start.9 = (bf16[32,256]{1,0:T(8,128)(2,1)S(1)}, bf16[32,256]{1,0:T(8,128)(2,1)}, u32[]{:S(2)}) copy-start(bf16[32,256]{1,0:T(8,128)(2,1)} %param.21) | copy-start | bytes 49156
  51.0 11.3 %all-to-all-start.4 = ((f32[32,2,8]{2,1,0:T(2,128)}), f32[32,2,8]{2,1,0:T(2,128)S(1)}, u32[]{:S(2)}, u32[]{:S(2)}) async-start(f32[32,2,8]{2,1,0:T(2,128)} %reshape.213), calls=%async_computation.4 | async-start | bytes 65536 | tf_op jit(solution)/shard_map/all_to_all | solution.py:102
  62.2 12.3 %all-to-all-start.3 = ((f32[32,2,8]{2,1,0:T(2,128)}), f32[32,2,8]{2,1,0:T(2,128)S(1)}, u32[]{:S(2)}, u32[]{:S(2)}) async-start(f32[32,2,8]{2,1,0:T(2,128)} %reshape.206), calls=%async_computation.3 | async-start | bytes 65536 | tf_op jit(solution)/shard_map/all_to_all | solution.py:95
  69.8 19.1 %copy-start.5 = (f32[32,2,4,160]{3,2,1,0:T(4,128)S(1)}, f32[32,2,4,160]{3,2,1,0:T(4,128)}, u32[]{:S(2)}) copy-start(f32[32,2,4,160]{3,2,1,0:T(4,128)} %copy-done.4) | copy-start | bytes 491524
  74.6 13.3 %all-to-all-start.2 = ((f32[32,2,1024]{2,1,0:T(2,128)}), f32[32,2,1024]{2,1,0:T(2,128)S(1)}, u32[]{:S(2)}, u32[]{:S(2)}) async-start(f32[32,2,1024]{2,1,0:T(2,128)} %reshape.204), calls=%async_computation.2 | async-start | bytes 524288 | tf_op jit(solution)/shard_map/all_to_all | solution.py:88
  78.9 53.7 %all-gather.6.cloned.1.call-start = ((), (), s32[]{:S(2)}) async-start(), calls=%async_computation.9 | async-start | bytes 3276800 | tf_op jit(solution)/shard_map/all_gather | solution.py:10
  98.3 38.3 %copy-start.7 = (f32[5120]{0:T(1024)S(1)}, f32[5120]{0:T(1024)}, u32[]{:S(2)}) copy-start(f32[5120]{0:T(1024)} %param.30) | copy-start | bytes 61444
  98.3 97.0 %all-gather.4.cloned.1.call-start = ((), (), s32[]{:S(2)}) async-start(), calls=%async_computation.7 | async-start | bytes 10813440 | tf_op jit(solution)/shard_map/all_gather | solution.py:163
  135.8 0.7 copy-start.3
  137.4 759.2 %reduce-scatter.2.cloned.1.call-start = ((), (), s32[]{:S(2)}) async-start(), calls=%async_computation.8 | async-start | bytes 21135360 | tf_op jit(solution)/shard_map/reduce_scatter | solution.py:178
  222.3 676.0 %copy-start.1 = (bf16[5120,256]{1,0:T(8,128)(2,1)S(1)}, bf16[5120,256]{1,0:T(8,128)(2,1)}, u32[]{:S(2)}) copy-start(bf16[5120,256]{1,0:T(8,128)(2,1)} %param.32) | copy-start | bytes 7864324
Sparse Core Ops, SparseCore 0:
  98.4 34.2 all-gather.5
  137.5 57.6 all-gather.3
  222.4 674.2 reduce-scatter.1
